TPU v7x, 32 devices: a whole 2x2x4 slice. The times are simulated.
32 devices in a mesh: store: 8 (over y, x, core), vocab: 4 (over z).
Axes of the slice: x: 2, y: 2, z: 4, core: 2. Of those that a mesh axis runs over, the one named last changes fastest.
Arguments:
- hidden: bfloat16 [512, 4096], P('store')
- lm_head: bfloat16 [4096, 65536], P(None, ('store', 'vocab'))
- store_keys: bfloat16 [8192, 4096], P(('store', 'vocab'))
- values: int32 [8192], P(('store', 'vocab')), may hold values from 0 to 65535, as said below
- licences: int32 [8192], P(('store', 'vocab')), may hold values from 0 to 29, as said below
- allowed: int32 [512], replicated, may hold values from 1 to 1073741823, as said below
Outputs:
- log_probs: float32 [512, 65536], P(None, ('store', 'vocab'))
Inputs may be any that keep to these rules, and one draw needn't show every extreme that they name: `values`: entry i holds a token t with t // 2048 = (i // 1024) * 4 + (i // 64) % 4: the entries of a device name tokens of the 8192 columns of its index along store, and its k-th run of 64 entries names tokens of the k-th 2048 columns of those. `licences`: some entry has licence 0. `allowed`: bit l of a position's word says whether licence l may be used; bit 0 is always set.
All inputs are finite; a program needn't handle non-finite values.
Results may differ from a plain program's by a relative error of at most 0.0003.
Values may be sent and summed in bfloat16 or wider, within the bound.
A program may use at most 128 MiB of HBM per device.

v0:
```python
import math
import jax
import jax.numpy as jnp
from jax import lax
from jax.sharding import PartitionSpec as P

NEG_FILL = -1e30


def mixture(lm_log, knn_mass, knn_total):
    share = knn_mass / knn_total[:, None]
    present = share > 0.0
    knn_log = jnp.where(present, jnp.log(jnp.where(present, share, 1.0)), -jnp.inf)
    return jnp.logaddexp(math.log(0.75) + lm_log, math.log(0.25) + knn_log)


def bin_tokens(weights, tokens, first_col, width):
    columns = lax.broadcasted_iota(jnp.int32, (tokens.shape[0], width), 1)
    token_table = ((tokens - first_col)[:, None] == columns).astype(jnp.float32)
    return jnp.dot(
        weights, token_table, precision=lax.Precision.HIGHEST, preferred_element_type=jnp.float32
    )


def body(hidden, lm_head, store_keys, values, licences, allowed):
    own_cols = lm_head.shape[1]
    inverse_root = 1.0 / math.sqrt(store_keys.shape[1])
    wide_keys = store_keys.astype(jnp.float32)
    key_half = 0.5 * jnp.sum(wide_keys * wide_keys, axis=1) * inverse_root
    portion = lax.all_gather(hidden, "store", axis=0, tiled=True)
    logit_rows = jnp.dot(portion, lm_head, preferred_element_type=jnp.float32)
    score_rows = lax.dot_general(
        portion, store_keys, (((1,), (1,)), ((), ())), preferred_element_type=jnp.float32
    )
    joined = jnp.concatenate([logit_rows, score_rows * inverse_root - key_half[None, :]], axis=1)
    logits = joined[:, :own_cols]
    scores = joined[:, own_cols:]
    permitted = jnp.bitwise_and(jnp.right_shift(allowed[:, None], licences[None, :]), 1) == 1
    masked = jnp.where(permitted, scores, NEG_FILL)
    lm_max, knn_max = lax.pmax(
        (jnp.max(logits, axis=1), jnp.max(masked, axis=1)), ("store", "vocab")
    )
    lm_terms = jnp.exp(logits - lm_max[:, None])
    kernel = jnp.where(permitted, jnp.exp(masked - knn_max[:, None]), 0.0)
    lm_total, knn_total = lax.psum(
        (jnp.sum(lm_terms, axis=1), jnp.sum(kernel, axis=1)), ("store", "vocab")
    )
    lm_log = logits - lm_max[:, None] - jnp.log(lm_total)[:, None]
    received, sources = (
        lax.all_to_all(
            kernel.astype(jnp.bfloat16), "vocab", split_axis=1, concat_axis=1, tiled=True
        ).astype(kernel.dtype),
        lax.all_to_all(values[None, :], "vocab", split_axis=1, concat_axis=1, tiled=True),
    )
    first_col = (
        lax.axis_index("store") * lax.axis_size("vocab") + lax.axis_index("vocab")
    ) * own_cols
    knn_mass = bin_tokens(received, sources[0], first_col, own_cols)
    return mixture(lm_log, knn_mass, knn_total)


def solution(mesh):
    return jax.shard_map(
        body,
        mesh=mesh,
        in_specs=(
            P("store", None),
            P(None, ("store", "vocab")),
            P(("store", "vocab"), None),
            P(("store", "vocab")),
            P(("store", "vocab")),
            P(),
        ),
        out_specs=P(None, ("store", "vocab")),
        check_vma=False,
    )
```

profile of v0, /device:TPU:0, one launch (start us, length us, event | category | flops | bytes accessed | tf_op | source)
XLA Modules:
  0.0 170.6 jit_solution(7530144514574135348)
XLA Ops:
  6.5 0.0 all-gather.2.cloned.1.call-start
  6.5 0.7 all-gather.2.cloned.1.call-update
  7.3 1.3 all_to_all.17
  8.6 6.3 %all-to-all-start.1 = ((s32[1,4,64]{2,0,1:T(1,128)}), s32[1,4,64]{2,0,1:T(1,128)S(1)}, u32[]{:S(2)}, u32[]{:S(2)}) async-start(s32[1,4,64]{2,0,1:T(1,128)} %all_to_all.17), calls=%async_computation.1 | async-start | bytes 4096 | tf_op jit(solution)/shard_map/all_to_all | solution.py:53
  14.9 2.1 %multiply_reduce_fusion = f32[256]{0:T(256)S(1)} fusion(bf16[256,4096]{1,0:T(8,128)(2,1)} %param.8), kind=kLoop, calls=%fused_computation.5 | loop fusion | flops 3145472 | bytes 2098176 | tf_op jit(solution)/shard_map/reduce_sum | solution.py:29
  17.0 0.0 copy-start
  17.0 0.0 copy-start.1
  17.0 0.0 copy-start.2
  17.0 31.7 %all-gather.2.cloned.1.call-done = bf16[512,4096]{1,0:T(8,128)(2,1)} async-done(((bf16[64,4096]{1,0:T(8,128)(2,1)}), bf16[512,4096]{1,0:T(8,128)(2,1)}) %all-gather.2.cloned.1.call-update) | async-done | bytes 4194320 | tf_op jit(solution)/shard_map/all_gather | solution.py:30
  48.7 0.0 copy-start.3
  48.7 17.1 %fusion.8 = (f32[512]{0:T(512)S(1)}, f32[512,2048]{1,0:T(8,128)}) fusion(bf16[512,4096]{1,0:T(8,128)(2,1)} %all-gather.2.cloned.1.call-done, bf16[4096,2048]{1,0:T(8,128)(2,1)} %param.7), kind=kOutput, calls=%fused_computation.20 | convolution fusion | flops 8590983168 | bytes 25167872 | tf_op jit(solution)/shard_map/dot_general | solution.py:31
  65.8 0.0 copy-done
  65.8 0.0 copy-done.1
  65.8 0.0 copy-done.2
  65.8 0.0 copy-done.3
  65.8 1.3 fusion.7
  67.1 39.4 %all-reduce.1 = (f32[512]{0:T(512)S(1)}, f32[512]{0:T(512)S(1)}) all-reduce(f32[512]{0:T(512)S(1)} %get-tuple-element.11, f32[512]{0:T(512)S(1)} %get-tuple-element.13), channel_id=1, replica_groups=mesh['store'=8,'vocab'=4] {'store','vocab'}, use_global_device_ids=true, to_apply=%region_6.7 | all-reduce | flops 1024 | bytes 8192 | tf_op jit(solution)/shard_map/pmax | solution.py:40
  106.5 0.9 fusion.5
  107.3 0.0 all-to-all-done.1
  107.3 3.6 %all-to-all-start = ((bf16[512,4,64]{0,2,1:T(8,128)(2,1)}), bf16[512,4,64]{0,2,1:T(8,128)(2,1)S(1)}, u32[]{:S(2)}, u32[]{:S(2)}) async-start(bf16[512,4,64]{0,2,1:T(8,128)(2,1)} %bitcast), calls=%async_computation | async-start | bytes 524288 | tf_op jit(solution)/shard_map/all_to_all | solution.py:50
  110.9 0.1 sub.62
  111.0 2.9 %exponential_reduce_fusion = f32[512]{0:T(512)S(1)} fusion(f32[512,2048]{1,0:T(8,128)} %get-tuple-element.14, f32[512]{0:T(512)S(1)} %get-tuple-element.8), kind=kLoop, calls=%fused_computation.7 | loop fusion | flops 2096640 | bytes 4198400 | tf_op jit(solution)/shard_map/reduce_sum | solution.py:46
  113.9 41.6 %all-reduce = (f32[512]{0:T(512)S(1)}, f32[512]{0:T(512)S(1)}) all-reduce(f32[512]{0:T(512)S(1)} %get-tuple-element.9, f32[512]{0:T(512)S(1)} %exponential_reduce_fusion), channel_id=1, replica_groups=mesh['store'=8,'vocab'=4] {'store','vocab'}, use_global_device_ids=true, to_apply=%region_8.9 | all-reduce | flops 1024 | bytes 8192 | tf_op jit(solution)/shard_map/psum | solution.py:45
  155.5 0.0 all-to-all-done
  155.5 8.2 %add_select_fusion = f32[512,2048]{1,0:T(8,128)} fusion(f32[512,2048]{1,0:T(8,128)} %get-tuple-element.14, bf16[512,256]{0,1:T(8,128)(2,1)S(1)} %bitcast.7, f32[512]{0:T(512)S(1)} %get-tuple-element.5, f32[512]{0:T(512)S(1)} %log.6, f32[512]{0:T(512)S(1)} %get-tuple-element.8, s32[256]{0:T(256)S(1)} %sub.62), kind=kOutput, calls=%fused_computation.4 | convolution fusion | flops 554172416 | bytes 8657920 | tf_op jit(solution)/shard_map/dot_general | solution.py:20
  (3 shorter events, 0.0 us)
Async XLA Ops:
  6.5 42.2 %all-gather.2.cloned.1.call-start = ((), (), s32[]{:S(2)}) async-start(), calls=%async_computation.2 | async-start | bytes 4718592 | tf_op jit(solution)/shard_map/all_gather | solution.py:30
  8.6 98.7 %all-to-all-start.1 = ((s32[1,4,64]{2,0,1:T(1,128)}), s32[1,4,64]{2,0,1:T(1,128)S(1)}, u32[]{:S(2)}, u32[]{:S(2)}) async-start(s32[1,4,64]{2,0,1:T(1,128)} %all_to_all.17), calls=%async_computation.1 | async-start | bytes 4096 | tf_op jit(solution)/shard_map/all_to_all | solution.py:53
  17.0 48.8 %copy-start = (bf16[256,4096]{1,0:T(8,128)(2,1)S(1)}, bf16[256,4096]{1,0:T(8,128)(2,1)}, u32[]{:S(2)}) copy-start(bf16[256,4096]{1,0:T(8,128)(2,1)} %param.8) | copy-start | bytes 6291460
  17.0 48.7 %copy-start.1 = (s32[512]{0:T(512)S(1)}, s32[512]{0:T(512)}, u32[]{:S(2)}) copy-start(s32[512]{0:T(512)} %param.11) | copy-start | bytes 6148
  17.0 48.7 %copy-start.2 = (s32[256]{0:T(256)S(1)}, s32[256]{0:T(256)}, u32[]{:S(2)}) copy-start(s32[256]{0:T(256)} %param.10) | copy-start | bytes 3076
  48.7 17.1 %copy-start.3 = (bf16[512,4096]{1,0:T(8,128)(2,1)S(1)}, bf16[512,4096]{1,0:T(8,128)(2,1)}, u32[]{:S(2)}) copy-start(bf16[512,4096]{1,0:T(8,128)(2,1)} %all-gather.2.cloned.1.call-done) | copy-start | bytes 12582916
  107.3 48.2 %all-to-all-start = ((bf16[512,4,64]{0,2,1:T(8,128)(2,1)}), bf16[512,4,64]{0,2,1:T(8,128)(2,1)S(1)}, u32[]{:S(2)}, u32[]{:S(2)}) async-start(bf16[512,4,64]{0,2,1:T(8,128)(2,1)} %bitcast), calls=%async_computation | async-start | bytes 524288 | tf_op jit(solution)/shard_map/all_to_all | solution.py:50
Sparse Core Ops, SparseCore 0:
  9.2 39.4 all-gather.1
where the time goes:
time: 171 us
  blocking collectives  81 us (47%)
  waiting for transfers between devices  32.4 us (19%)
  matrix products  26.6 us (16%)
  between operations  13.4 us (8%)
  starting transfers between devices  9.87 us (6%)
  other arithmetic  5.86 us (3%)
    psum x1, blocking collectives, body(): lax.psum((jnp.sum(lm_terms, axis=1), jnp.sum(kernel, axis=1)), ('store',...  41.6 us
    pmax x1, blocking collectives, body(): lax.pmax((jnp.max(logits, axis=1), jnp.max(masked, axis=1)), ('store', 'v...  39.4 us
    all_gather x1, waiting for transfers between devices, body(): portion = lax.all_gather(hidden, 'store', axis=0, tiled=True)  31.7 us
    dot_general x1, matrix products, body(): logit_rows = jnp.dot(portion, lm_head, preferred_element_type=jnp.float32)  17.1 us
    dot_general x1, matrix products, bin_tokens(): jnp.dot(weights, token_table, precision=lax.Precision.HIGHEST, preferred_...  8.19 us
    all_to_all x1, starting transfers between devices, body(): lax.all_to_all(values[None, :], 'vocab', split_axis=1, concat_axis=1, til...  6.32 us
    all_to_all x1, starting transfers between devices, body(): lax.all_to_all(kernel.astype(jnp.bfloat16), 'vocab', split_axis=1, concat...  3.55 us
  transfers between devices with their start and end apart: 3, of which 1 were waited for; matrix products, arithmetic and copies ran while one was open for 14% of the time, Pallas kernels for 0%

commit v1 on v0

--- a/solution.py
+++ b/solution.py
@@ -27,7 +27,19 @@
     inverse_root = 1.0 / math.sqrt(store_keys.shape[1])
     wide_keys = store_keys.astype(jnp.float32)
     key_half = 0.5 * jnp.sum(wide_keys * wide_keys, axis=1) * inverse_root
-    portion = lax.all_gather(hidden, "store", axis=0, tiled=True)
+    many = lax.axis_size("store")
+    lanes = [(c, (c + 1) % many) for c in range(many)]
+    by_rank = [(c, (c - 1) % many) for c in range(many)]
+    shaped, part_now = ([hidden], [hidden])
+    for _ in range(many // 2):
+        oldest = lax.ppermute(shaped[-1], "store", lanes)
+        shaped.append(oldest)
+    for _ in range((many - 1) // 2):
+        res = lax.ppermute(part_now[-1], "store", by_rank)
+        part_now.append(res)
+    lower = jnp.concatenate([*shaped[::-1], *part_now[1:]], 0)
+    inter = lax.axis_index("store")
+    portion = jnp.roll(lower, shift=(inter - many // 2) * hidden.shape[0], axis=0)
     logit_rows = jnp.dot(portion, lm_head, preferred_element_type=jnp.float32)
     score_rows = lax.dot_general(
         portion, store_keys, (((1,), (1,)), ((), ())), preferred_element_type=jnp.float32

time: 171 us -> 172 us (level)
  between operations: 13.4 us -> 0.17 us
  starting transfers between devices: 9.87 us -> 18.8 us
  local copies, waits for them, and re-layouts: 1.45 us -> 5.16 us
  waiting for transfers between devices: 32.4 us -> 36 us
  matrix products: 26.6 us -> 23.6 us
    ppermute x0 -> x7, waiting for transfers between devices: none -> 36 us  [the longest x4 31.7 us: body(): oldest = lax.ppermute(shaped[-1], 'store', lanes)]
    all_gather x1 -> x0, waiting for transfers between devices: 31.7 us -> none  [body(): portion = lax.all_gather(hidden, 'store', axis=0, tiled=True)]
    ppermute x0 -> x7, starting transfers between devices: none -> 8.16 us  [the longest x3 7.7 us: body(): res = lax.ppermute(part_now[-1], 'store', by_rank)]
    unnamed x8 -> x23, local copies, waits for them, and re-layouts: 0.02 us -> 3.69 us
    dot_general x1, matrix products: 17.1 us -> 14.1 us  [body(): logit_rows = jnp.dot(portion, lm_head, preferred_element_type=jnp.float32)]
    pmax x1, blocking collectives: 39.4 us -> 41.6 us  [body(): lax.pmax((jnp.max(logits, axis=1), jnp.max(masked, axis=1)), ('store', 'v...]
  transfers between devices with their start and end apart: 3 -> 9, of which waited for: 1 -> 4; matrix products, arithmetic and copies ran while one was open for 14% -> 15% of each run, Pallas kernels for 0% -> 0%
where the time goes in v1:
time: 172 us
  blocking collectives  82.2 us (48%)
  waiting for transfers between devices  36 us (21%)
  matrix products  23.6 us (14%)
  starting transfers between devices  18.8 us (11%)
  other arithmetic  5.86 us (3%)
  local copies, waits for them, and re-layouts  5.16 us (3%)
    pmax x1, blocking collectives, body(): lax.pmax((jnp.max(logits, axis=1), jnp.max(masked, axis=1)), ('store', 'v...  41.6 us
    psum x1, blocking collectives, body(): lax.psum((jnp.sum(lm_terms, axis=1), jnp.sum(kernel, axis=1)), ('store',...  40.6 us
    ppermute x4, waiting for transfers between devices, body(): oldest = lax.ppermute(shaped[-1], 'store', lanes)  31.7 us
    dot_general x1, matrix products, body(): logit_rows = jnp.dot(portion, lm_head, preferred_element_type=jnp.float32)  14.1 us
    dot_general x1, matrix products, bin_tokens(): jnp.dot(weights, token_table, precision=lax.Precision.HIGHEST, preferred_...  8.21 us
    ppermute x3, starting transfers between devices, body(): res = lax.ppermute(part_now[-1], 'store', by_rank)  7.7 us
    all_to_all x1, starting transfers between devices, body(): lax.all_to_all(values[None, :], 'vocab', split_axis=1, concat_axis=1, til...  7.11 us
    ppermute x3, waiting for transfers between devices, body(): res = lax.ppermute(part_now[-1], 'store', by_rank)  4.32 us
  transfers between devices with their start and end apart: 9, of which 4 were waited for; matrix products, arithmetic and copies ran while one was open for 15% of the time, Pallas kernels for 0%

profile of v1, /device:TPU:0, one launch (start us, length us, event | category | flops | bytes accessed | tf_op | source)
XLA Modules:
  0.0 171.9 jit_solution(1013120917859300901)
XLA Ops:
  0.0 0.0 copy-start.1
  0.0 0.5 collective-permute-start
  0.5 10.0 %collective-permute-done = bf16[64,4096]{1,0:T(8,128)(2,1)S(1)} collective-permute-done((bf16[64,4096]{1,0:T(8,128)(2,1)}, bf16[64,4096]{1,0:T(8,128)(2,1)S(1)}, u32[]{:S(2)}, u32[]{:S(2)}) %collective-permute-start) | collective-permute-done | bytes 524320 | tf_op jit(solution)/shard_map/ppermute | solution.py:35
  10.5 0.0 collective-permute-start.1
  10.5 2.6 %collective-permute-start.4 = (bf16[64,4096]{1,0:T(8,128)(2,1)}, bf16[64,4096]{1,0:T(8,128)(2,1)S(1)}, u32[]{:S(2)}, u32[]{:S(2)}) collective-permute-start(bf16[64,4096]{1,0:T(8,128)(2,1)} %param.6), channel_id=1, source_target_pairs={{0,28},{4,0},{8,4},{12,8},{16,12},{20,16},{24,20},{28,24},{1,29},{... | collective-permute-start | bytes 1572872 | tf_op jit(solution)/shard_map/ppermute | solution.py:38
  13.1 10.6 %collective-permute-done.1 = bf16[64,4096]{1,0:T(8,128)(2,1)S(1)} collective-permute-done((bf16[64,4096]{1,0:T(8,128)(2,1)S(1)}, bf16[64,4096]{1,0:T(8,128)(2,1)S(1)}, u32[]{:S(2)}, u32[]{:S(2)}) %collective-permute-start.1) | collective-permute-done | bytes 524320 | tf_op jit(solution)/shard_map/ppermute | solution.py:35
  23.7 0.0 collective-permute-start.2
  23.7 0.0 collective-permute-done.4
  23.7 2.6 %collective-permute-start.5 = (bf16[64,4096]{1,0:T(8,128)(2,1)S(1)}, bf16[64,4096]{1,0:T(8,128)(2,1)S(1)}, u32[]{:S(2)}, u32[]{:S(2)}) collective-permute-start(bf16[64,4096]{1,0:T(8,128)(2,1)S(1)} %collective-permute-done.4), channel_id=1, source_target_pairs={{0,28},{4,0},{8,4},{12,8},{16,12},{20,16},{24,20},{28,24},{1,29},{... | collective-permute-start | bytes 1572872 | tf_op jit(solution)/shard_map/ppermute | solution.py:38
  26.3 11.1 %collective-permute-done.2 = bf16[64,4096]{1,0:T(8,128)(2,1)S(1)} collective-permute-done((bf16[64,4096]{1,0:T(8,128)(2,1)S(1)}, bf16[64,4096]{1,0:T(8,128)(2,1)S(1)}, u32[]{:S(2)}, u32[]{:S(2)}) %collective-permute-start.2) | collective-permute-done | bytes 524320 | tf_op jit(solution)/shard_map/ppermute | solution.py:35
  37.5 0.0 collective-permute-start.3
  37.5 1.4 all_to_all.17
  38.8 7.1 %all-to-all-start.1 = ((s32[1,4,64]{2,0,1:T(1,128)}), s32[1,4,64]{2,0,1:T(1,128)S(1)}, u32[]{:S(2)}, u32[]{:S(2)}) async-start(s32[1,4,64]{2,0,1:T(1,128)} %all_to_all.17), calls=%async_computation.1 | async-start | bytes 4096 | tf_op jit(solution)/shard_map/all_to_all | solution.py:65
  45.9 2.1 %multiply_reduce_fusion = f32[256]{0:T(256)S(1)} fusion(bf16[256,4096]{1,0:T(8,128)(2,1)} %param.8), kind=kLoop, calls=%fused_computation.5 | loop fusion | flops 3145472 | bytes 2098176 | tf_op jit(solution)/shard_map/reduce_sum | solution.py:29
  48.0 0.0 collective-permute-done.5
  48.0 2.4 %collective-permute-start.6 = (bf16[64,4096]{1,0:T(8,128)(2,1)S(1)}, bf16[64,4096]{1,0:T(8,128)(2,1)S(1)}, u32[]{:S(2)}, u32[]{:S(2)}) collective-permute-start(bf16[64,4096]{1,0:T(8,128)(2,1)S(1)} %collective-permute-done.5), channel_id=1, source_target_pairs={{0,28},{4,0},{8,4},{12,8},{16,12},{20,16},{24,20},{28,24},{1,29},{... | collective-permute-start | bytes 1572872 | tf_op jit(solution)/shard_map/ppermute | solution.py:38
  50.5 0.0 collective-permute-done.3
  50.5 1.1 constant_dynamic-update-slice_fusion.15
  51.7 1.1 constant_dynamic-update-slice_fusion.11
  52.8 4.3 %collective-permute-done.6 = bf16[64,4096]{1,0:T(8,128)(2,1)S(1)} collective-permute-done((bf16[64,4096]{1,0:T(8,128)(2,1)S(1)}, bf16[64,4096]{1,0:T(8,128)(2,1)S(1)}, u32[]{:S(2)}, u32[]{:S(2)}) %collective-permute-start.6) | collective-permute-done | bytes 524320 | tf_op jit(solution)/shard_map/ppermute | solution.py:38
  57.2 1.1 constant_dynamic-update-slice_fusion.7
  58.4 0.0 copy-done.1
  58.6 0.0 copy-start
  58.6 0.0 copy-start.2
  58.6 0.0 copy-start.3
  58.6 14.1 %fusion.21 = (f32[512]{0:T(512)S(1)}, f32[512,2048]{1,0:T(8,128)}) fusion(bf16[4096,2048]{1,0:T(8,128)(2,1)} %param.7, bf16[1024,4096]{1,0:T(8,128)(2,1)S(1)} %constant_dynamic-update-slice_fusion, s32[]{:T(128)S(6)} %select_n.31), kind=kOutput, calls=%fused_computation.42 | convolution fusion | flops 8590983168 | bytes 25167876 | tf_op jit(solution)/shard_map/dot_general | solution.py:43
  72.7 0.0 copy-done
  72.7 0.0 copy-done.2
  72.7 0.0 copy-done.3
  72.7 1.3 fusion.20
  74.0 41.6 %all-reduce.1 = (f32[512]{0:T(512)S(1)}, f32[512]{0:T(512)S(1)}) all-reduce(f32[512]{0:T(512)S(1)} %get-tuple-element.11, f32[512]{0:T(512)S(1)} %get-tuple-element.13), channel_id=1, replica_groups=mesh['store'=8,'vocab'=4] {'store','vocab'}, use_global_device_ids=true, to_apply=%region_6.7 | all-reduce | flops 1024 | bytes 8192 | tf_op jit(solution)/shard_map/pmax | solution.py:52
  115.6 0.9 fusion.16
  116.5 0.0 all-to-all-done.1
  116.5 3.6 %all-to-all-start = ((bf16[512,4,64]{0,2,1:T(8,128)(2,1)}), bf16[512,4,64]{0,2,1:T(8,128)(2,1)S(1)}, u32[]{:S(2)}, u32[]{:S(2)}) async-start(bf16[512,4,64]{0,2,1:T(8,128)(2,1)} %bitcast), calls=%async_computation | async-start | bytes 524288 | tf_op jit(solution)/shard_map/all_to_all | solution.py:62
  120.1 0.1 sub.71
  120.2 2.9 %exponential_reduce_fusion = f32[512]{0:T(512)S(1)} fusion(f32[512,2048]{1,0:T(8,128)} %get-tuple-element.14, f32[512]{0:T(512)S(1)} %get-tuple-element.8), kind=kLoop, calls=%fused_computation.7 | loop fusion | flops 2096640 | bytes 4198400 | tf_op jit(solution)/shard_map/reduce_sum | solution.py:58
  123.1 40.6 %all-reduce = (f32[512]{0:T(512)S(1)}, f32[512]{0:T(512)S(1)}) all-reduce(f32[512]{0:T(512)S(1)} %get-tuple-element.9, f32[512]{0:T(512)S(1)} %exponential_reduce_fusion), channel_id=1, replica_groups=mesh['store'=8,'vocab'=4] {'store','vocab'}, use_global_device_ids=true, to_apply=%region_8.9 | all-reduce | flops 1024 | bytes 8192 | tf_op jit(solution)/shard_map/psum | solution.py:57
  163.7 0.0 all-to-all-done
  163.7 8.2 %add_select_fusion = f32[512,2048]{1,0:T(8,128)} fusion(f32[512,2048]{1,0:T(8,128)} %get-tuple-element.14, bf16[512,256]{0,1:T(8,128)(2,1)S(1)} %bitcast.5, f32[512]{0:T(512)S(1)} %get-tuple-element.5, f32[512]{0:T(512)S(1)} %log.6, f32[512]{0:T(512)S(1)} %get-tuple-element.8, s32[256]{0:T(256)S(1)} %sub.71), kind=kOutput, calls=%fused_computation.4 | convolution fusion | flops 554172416 | bytes 8657920 | tf_op jit(solution)/shard_map/dot_general | solution.py:20
  (16 shorter events, 0.5 us)
Async XLA Ops:
  0.0 58.4 %copy-start.1 = (bf16[64,4096]{1,0:T(8,128)(2,1)S(1)}, bf16[64,4096]{1,0:T(8,128)(2,1)}, u32[]{:S(2)}) copy-start(bf16[64,4096]{1,0:T(8,128)(2,1)} %param.6) | copy-start | bytes 1572868
  0.0 10.5 %collective-permute-start = (bf16[64,4096]{1,0:T(8,128)(2,1)}, bf16[64,4096]{1,0:T(8,128)(2,1)S(1)}, u32[]{:S(2)}, u32[]{:S(2)}) collective-permute-start(bf16[64,4096]{1,0:T(8,128)(2,1)} %param.6), channel_id=1, source_target_pairs={{0,4},{4,8},{8,12},{12,16},{16,20},{20,24},{24,28},{28,0},{1,5},{5... | collective-permute-start | bytes 1572872 | tf_op jit(solution)/shard_map/ppermute | solution.py:35
  10.5 13.2 %collective-permute-start.1 = (bf16[64,4096]{1,0:T(8,128)(2,1)S(1)}, bf16[64,4096]{1,0:T(8,128)(2,1)S(1)}, u32[]{:S(2)}, u32[]{:S(2)}) collective-permute-start(bf16[64,4096]{1,0:T(8,128)(2,1)S(1)} %collective-permute-done), channel_id=1, source_target_pairs={{0,4},{4,8},{8,12},{12,16},{16,20},{20,24},{24,28},{28,0},{1,5},{5... | collective-permute-start | bytes 1572872 | tf_op jit(solution)/shard_map/ppermute | solution.py:35
  10.5 13.2 %collective-permute-start.4 = (bf16[64,4096]{1,0:T(8,128)(2,1)}, bf16[64,4096]{1,0:T(8,128)(2,1)S(1)}, u32[]{:S(2)}, u32[]{:S(2)}) collective-permute-start(bf16[64,4096]{1,0:T(8,128)(2,1)} %param.6), channel_id=1, source_target_pairs={{0,28},{4,0},{8,4},{12,8},{16,12},{20,16},{24,20},{28,24},{1,29},{... | collective-permute-start | bytes 1572872 | tf_op jit(solution)/shard_map/ppermute | solution.py:38
  23.7 13.8 %collective-permute-start.2 = (bf16[64,4096]{1,0:T(8,128)(2,1)S(1)}, bf16[64,4096]{1,0:T(8,128)(2,1)S(1)}, u32[]{:S(2)}, u32[]{:S(2)}) collective-permute-start(bf16[64,4096]{1,0:T(8,128)(2,1)S(1)} %collective-permute-done.1), channel_id=1, source_target_pairs={{0,4},{4,8},{8,12},{12,16},{16,20},{20,24},{24,28},{28,0},{1,5},{5... | collective-permute-start | bytes 1572872 | tf_op jit(solution)/shard_map/ppermute | solution.py:35
  23.7 24.3 %collective-permute-start.5 = (bf16[64,4096]{1,0:T(8,128)(2,1)S(1)}, bf16[64,4096]{1,0:T(8,128)(2,1)S(1)}, u32[]{:S(2)}, u32[]{:S(2)}) collective-permute-start(bf16[64,4096]{1,0:T(8,128)(2,1)S(1)} %collective-permute-done.4), channel_id=1, source_target_pairs={{0,28},{4,0},{8,4},{12,8},{16,12},{20,16},{24,20},{28,24},{1,29},{... | collective-permute-start | bytes 1572872 | tf_op jit(solution)/shard_map/ppermute | solution.py:38
  37.5 13.0 %collective-permute-start.3 = (bf16[64,4096]{1,0:T(8,128)(2,1)S(1)}, bf16[64,4096]{1,0:T(8,128)(2,1)}, u32[]{:S(2)}, u32[]{:S(2)}) collective-permute-start(bf16[64,4096]{1,0:T(8,128)(2,1)S(1)} %collective-permute-done.2), channel_id=1, source_target_pairs={{0,4},{4,8},{8,12},{12,16},{16,20},{20,24},{24,28},{28,0},{1,5},{5... | collective-permute-start | bytes 1572872 | tf_op jit(solution)/shard_map/ppermute | solution.py:35
  38.8 77.7 %all-to-all-start.1 = ((s32[1,4,64]{2,0,1:T(1,128)}), s32[1,4,64]{2,0,1:T(1,128)S(1)}, u32[]{:S(2)}, u32[]{:S(2)}) async-start(s32[1,4,64]{2,0,1:T(1,128)} %all_to_all.17), calls=%async_computation.1 | async-start | bytes 4096 | tf_op jit(solution)/shard_map/all_to_all | solution.py:65
  48.0 9.1 %collective-permute-start.6 = (bf16[64,4096]{1,0:T(8,128)(2,1)S(1)}, bf16[64,4096]{1,0:T(8,128)(2,1)S(1)}, u32[]{:S(2)}, u32[]{:S(2)}) collective-permute-start(bf16[64,4096]{1,0:T(8,128)(2,1)S(1)} %collective-permute-done.5), channel_id=1, source_target_pairs={{0,28},{4,0},{8,4},{12,8},{16,12},{20,16},{24,20},{28,24},{1,29},{... | collective-permute-start | bytes 1572872 | tf_op jit(solution)/shard_map/ppermute | solution.py:38
  58.6 14.1 %copy-start = (bf16[256,4096]{1,0:T(8,128)(2,1)S(1)}, bf16[256,4096]{1,0:T(8,128)(2,1)}, u32[]{:S(2)}) copy-start(bf16[256,4096]{1,0:T(8,128)(2,1)} %param.8) | copy-start | bytes 6291460
  58.6 14.1 %copy-start.2 = (s32[512]{0:T(512)S(1)}, s32[512]{0:T(512)}, u32[]{:S(2)}) copy-start(s32[512]{0:T(512)} %param.11) | copy-start | bytes 6148
  58.6 14.1 %copy-start.3 = (s32[256]{0:T(256)S(1)}, s32[256]{0:T(256)}, u32[]{:S(2)}) copy-start(s32[256]{0:T(256)} %param.10) | copy-start | bytes 3076
  116.5 47.2 %all-to-all-start = ((bf16[512,4,64]{0,2,1:T(8,128)(2,1)}), bf16[512,4,64]{0,2,1:T(8,128)(2,1)S(1)}, u32[]{:S(2)}, u32[]{:S(2)}) async-start(bf16[512,4,64]{0,2,1:T(8,128)(2,1)} %bitcast), calls=%async_computation | async-start | bytes 524288 | tf_op jit(solution)/shard_map/all_to_all | solution.py:62
